TPU v7x, 512 devices: a whole 4x4x16 slice. The times are simulated.
512 devices in a mesh: tile: 128 (over z, y, core), scan: 4 (over x).
Axes of the slice: x: 4, y: 4, z: 16, core: 2. Of those that a mesh axis runs over, the one named last changes fastest.
Arguments:
- object_slab: float32 [2, 2, 8192, 512], P(None, None, 'tile', 'scan'), may hold values from -6 to 6
- probe_wave: bfloat16 [2, 512, 512], P(None, None, 'scan'), may hold values from -6 to 6
- amplitudes: float32 [256, 512, 512], P('tile', 'scan'), may hold values from 0.2 to 2
- row_offsets: int32 [256], P('tile'), may hold values from 0 to 63
- position_counts: int32 [128], P('tile'), may hold values from 0 to 2, as said below
Outputs:
- object_grad: float32 [2, 2, 8192, 512], P(None, None, 'tile', 'scan')
Inputs may be any that keep to these rules, and one draw needn't show every extreme that they name: position_counts is 1 to 2 on the first 120 tiles, equal to 2 on at least one of them, and 0 on the last 8 tiles.
All inputs are finite; a program needn't handle non-finite values.
Results may differ from a plain program's by a relative error of at most 0.0065.
Values may be sent and summed in bfloat16 or wider, within the bound.
A program may use at most 64 MiB of HBM per device.

v0:
```python
import functools
import math

import jax
import jax.numpy as jnp
import numpy as np
from jax import lax
from jax.experimental import pallas as pl
from jax.experimental.pallas import tpu as pltpu
from jax.sharding import PartitionSpec as P

P_SIZE = 512
HALF = 256
BLK = 128
TH = 64
SPAN = P_SIZE // TH

fresnel = 0.5
smooth = 1.0
MESH = pl.DeviceIdType.MESH
BF = jnp.bfloat16
F32 = jnp.float32


def tables():
    index = np.arange(P_SIZE)
    angles = 2.0 * np.pi / P_SIZE * (index[:, None] * index[None, :] % P_SIZE)
    wave = np.exp(1j * angles)
    far = np.conj(wave) / math.sqrt(P_SIZE)
    centred = np.where(index < P_SIZE // 2, index, index - P_SIZE).astype(np.float64)
    kernel = np.exp(-1j * np.pi * fresnel / P_SIZE * centred * centred)
    near = (wave * kernel[None, :]) @ np.conj(wave).T / P_SIZE

    def planes(table):
        both = np.stack([table.real, table.imag])
        return both.astype(np.float32).astype(BF)

    return planes(far), planes(near)


def body(
    tiles,
    off_ref, cnt_ref, slab_hbm, probe_hbm, amp_hbm, tq_hbm, tf_hbm,
    out_ref,
    slab, probe, ampf, aq, bq, af, bf,
    stage, win, sel, put, h1, o2p, ampb, hr, o2r, amp,
    ps, ew, gs, x1, ch, ks, y, t2s, gw, b2s, b2r, t2r, tp, outs, oin,
    loc_sem, tab_sem,
    in_ss, in_rs, h1_ss, h1_rs, o2_ss, o2_rs, am_ss, am_rs,
    e1_ss, e1_rs, e2_ss, e2_rs, b2_ss, b2_rs, t2_ss, t2_rs, out_ss, out_rs,
):
    t = lax.axis_index("tile")
    x = lax.axis_index("scan")
    c = lax.rem(t, 2)
    d = 1 - c
    pair = t - c
    home = pair + x // 2
    slot = lax.rem(x, 2)

    def remote(src, dst, ss, rs, tile, scan):
        return pltpu.make_async_remote_copy(
            src_ref=src, dst_ref=dst, send_sem=ss, recv_sem=rs,
            device_id={"tile": tile, "scan": scan}, device_id_type=MESH,
        )

    barrier = pltpu.get_barrier_semaphore()

    def greet(tile, scan):
        pl.semaphore_signal(
            barrier, inc=1, device_id={"tile": tile, "scan": scan}, device_id_type=MESH
        )

    for k in range(1, SPAN + 1):
        greet(lax.rem(t + k, tiles), x)
        greet(lax.rem(t + tiles - k, tiles), x)
    for step in range(1, 4):
        for core in range(2):
            greet(pair + core, lax.rem(x + step, 4))

    loads = [
        pltpu.make_async_copy(slab_hbm, slab, loc_sem.at[0]),
        pltpu.make_async_copy(amp_hbm, ampf, loc_sem.at[1]),
        pltpu.make_async_copy(probe_hbm, probe, loc_sem.at[2]),
    ]
    for load in loads:
        load.start()

    def table_loads(src, dst, which, column):
        copies = []
        for n, (up, left, plane) in enumerate([(0, 0, 0), (1 - column, column, 1), (1, 1, 0)]):
            where = dst.at[pl.ds(up * P_SIZE, P_SIZE), pl.ds(left * P_SIZE, P_SIZE)]
            copies.append(pltpu.make_async_copy(src.at[plane], where, tab_sem.at[which, n]))
        for copy in copies:
            copy.start()
        return copies

    def table_ready(dst, copies, column):
        for copy in copies:
            copy.wait()
        imag = dst[(1 - column) * P_SIZE:(2 - column) * P_SIZE, column * P_SIZE:(column + 1) * P_SIZE]
        dst[column * P_SIZE:(column + 1) * P_SIZE, (1 - column) * P_SIZE:(2 - column) * P_SIZE] = -imag

    aq_loads = table_loads(tq_hbm, aq, 0, 0)
    bq_loads = table_loads(tq_hbm, bq, 1, 1)
    bf_loads = table_loads(tf_hbm, bf, 2, 1)
    af_loads = table_loads(tf_hbm, af, 3, 0)

    loads[0].wait()
    for s in range(2):
        for part in range(2):
            piece = slab[s, part].astype(BF)
            stage[s, :, part * BLK:(part + 1) * BLK] = piece
            win[s, 0, :, part * BLK:(part + 1) * BLK] = piece
    loads[1].wait()
    for s in range(2):
        for r in range(2):
            ampb[s, r] = ampf[s, :, r * HALF:(r + 1) * HALF].astype(BF)
    for s in range(2):
        shape = (P_SIZE, P_SIZE + TH)
        shifted = lax.broadcasted_iota(jnp.int32, shape, 0) + off_ref[s]
        match = shifted == lax.broadcasted_iota(jnp.int32, shape, 1)
        sel[s] = jnp.where(match, 1.0, 0.0).astype(BF)
        shape = (P_SIZE + TH, P_SIZE)
        shifted = lax.broadcasted_iota(jnp.int32, shape, 1) + off_ref[s]
        match = shifted == lax.broadcasted_iota(jnp.int32, shape, 0)
        alive = jnp.broadcast_to(cnt_ref[0], shape) > s
        put[:, s * P_SIZE:(s + 1) * P_SIZE] = jnp.where(
            jnp.logical_and(match, alive), 1.0, 0.0).astype(BF)

    pl.semaphore_wait(barrier, 2 * SPAN + 6)

    sends = []
    for s in range(2):
        for k in range(1, SPAN + 1):
            copy = remote(
                stage.at[s], win.at[s, k], in_ss.at[s, k], in_rs.at[s, k],
                lax.rem(t + tiles - k, tiles), x,
            )
            copy.start()
            sends.append(copy)

    def is_self(s, r):
        return jnp.logical_and(2 * c + s == x, c == r)

    def spread(src, dst, ss, rs, s, r):
        mine = is_self(s, r)

        @pl.when(mine)
        def _():
            pltpu.make_async_copy(src, dst.at[x], rs.at[x]).start()

        @pl.when(jnp.logical_not(mine))
        def _():
            remote(src, dst.at[x], ss.at[s, r], rs.at[x], pair + r, 2 * c + s).start()

    def spread_wait(src, dst, ss, rs, s, r):
        @pl.when(jnp.logical_not(is_self(s, r)))
        def _():
            remote(src, dst.at[x], ss.at[s, r], rs.at[x], pair + r, 2 * c + s).wait_send()

    def amp_of(s, r):
        return ampb.at[s, r], amp, am_ss, am_rs, s, r

    def h1_of(s, r):
        return h1.at[s, :, pl.ds(r * HALF, HALF), :], hr, h1_ss, h1_rs, s, r

    def o2_of(s, r):
        return o2p.at[s, :, pl.ds(r * HALF, HALF), :], o2r, o2_ss, o2_rs, s, r

    for s in range(2):
        for r in range(2):
            spread(*amp_of(s, r))

    table_ready(aq, aq_loads, 0)
    table_ready(bq, bq_loads, 1)
    table_ready(bf, bf_loads, 1)
    table_ready(af, af_loads, 0)

    def receive(dst, rs):
        pltpu.make_async_copy(dst, dst, rs).wait()

    def window(s):
        for k in range(1, SPAN + 1):
            receive(win.at[s, k], in_rs.at[s, k])
        return jnp.concatenate([win[s, k] for k in range(SPAN + 1)], axis=0)

    def dot(left, right):
        return jnp.dot(left, right, preferred_element_type=F32)

    loads[2].wait()
    wide = window(0)
    psi = []
    for s in range(2):
        patch = dot(sel[s], wide)
        pr, pi = probe[0].astype(F32), probe[1].astype(F32)
        fr, fi = patch[:, :BLK], patch[:, BLK:]
        psi.append(jnp.concatenate([
            (pr * fr - pi * fi).astype(BF), (pr * fi + pi * fr).astype(BF)], axis=0))
    psi = jnp.concatenate(psi, axis=1)
    for r in range(2):
        for part in range(2):
            at = part * P_SIZE + r * HALF
            half1 = dot(aq[at:at + HALF, :], psi).astype(BF)
            for s in range(2):
                h1[s, part, r * HALF:(r + 1) * HALF, :] = half1[:, s * BLK:(s + 1) * BLK]
        for s in range(2):
            spread(*h1_of(s, r))

    wide = window(1)
    for s in range(2):
        patch = dot(sel[s], wide).astype(BF)
        for part in range(2):
            o2p[s, part] = patch[:, part * BLK:(part + 1) * BLK]
        for r in range(2):
            spread(*o2_of(s, r))

    for n in range(4):
        receive(hr.at[n], h1_rs.at[n])
    left = jnp.concatenate([hr[n, part] for part in range(2) for n in range(4)], axis=1)
    for part in range(2):
        for h in range(2):
            at = part * P_SIZE + h * HALF
            ps[part, h] = dot(left, bq[:, at:at + HALF]).astype(BF)
    for n in range(4):
        receive(o2r.at[n], o2_rs.at[n])

    def second(part, h):
        return jnp.concatenate([o2r[2 * h, part], o2r[2 * h + 1, part]], axis=1).astype(F32)

    for h in range(2):
        wr, wi = ps[0, h].astype(F32), ps[1, h].astype(F32)
        sr, si = second(0, h), second(1, h)
        ew[:, h * HALF:(h + 1) * HALF] = (wr * sr - wi * si).astype(BF)
        ew[:, P_SIZE + h * HALF:P_SIZE + (h + 1) * HALF] = (wr * si + wi * sr).astype(BF)

    for part in range(2):
        at = pl.multiple_of(part * P_SIZE + d * HALF, HALF)
        gs[part] = dot(ew[...], bf[:, pl.ds(at, HALF)]).astype(BF)
    ex1 = remote(gs, x1.at[c], e1_ss, e1_rs, pair + d, x)
    ex1.start()
    for part in range(2):
        at = pl.multiple_of(part * P_SIZE + c * HALF, HALF)
        x1[c, part] = dot(ew[...], bf[:, pl.ds(at, HALF)]).astype(BF)
    for n in range(4):
        receive(amp.at[n], am_rs.at[n])
    receive(x1.at[d], e1_rs)

    right = jnp.concatenate([x1[r, part] for part in range(2) for r in range(2)], axis=0)
    for r in range(2):
        fr = dot(af[r * HALF:(r + 1) * HALF, :], right)
        fi = dot(af[P_SIZE + r * HALF:P_SIZE + (r + 1) * HALF, :], right)
        measured = jnp.concatenate([amp[2 * r], amp[2 * r + 1]], axis=0).astype(F32)
        keeping = 1.0 - measured / jnp.sqrt(fr * fr + fi * fi + smooth)
        ch[r * HALF:(r + 1) * HALF, :] = (fr * keeping).astype(BF)
        ch[P_SIZE + r * HALF:P_SIZE + (r + 1) * HALF, :] = (fi * keeping).astype(BF)

    for part in range(2):
        at = pl.multiple_of(part * P_SIZE + d * HALF, HALF)
        ks[part] = dot(bf[pl.ds(at, HALF), :], ch[...]).astype(BF)
    ex2 = remote(ks, y.at[c], e2_ss, e2_rs, pair + d, x)
    ex2.start()
    for part in range(2):
        at = pl.multiple_of(part * P_SIZE + c * HALF, HALF)
        y[c, part] = dot(bf[pl.ds(at, HALF), :], ch[...]).astype(BF)
    receive(y.at[d], e2_rs)

    left = jnp.concatenate([y[h, part] for part in range(2) for h in range(2)], axis=1)
    for h in range(2):
        er = dot(left, af[:, h * HALF:(h + 1) * HALF])
        ei = dot(left, af[:, P_SIZE + h * HALF:P_SIZE + (h + 1) * HALF])
        wr, wi = ps[0, h].astype(F32), ps[1, h].astype(F32)
        sr, si = second(0, h), second(1, h)
        tr, ti = (wr * er + wi * ei).astype(BF), (wr * ei - wi * er).astype(BF)
        for n in range(2):
            t2s[2 * h + n, 0] = tr[:, n * BLK:(n + 1) * BLK]
            t2s[2 * h + n, 1] = ti[:, n * BLK:(n + 1) * BLK]
        gw[:, h * HALF:(h + 1) * HALF] = (sr * er + si * ei).astype(BF)
        gw[:, P_SIZE + h * HALF:P_SIZE + (h + 1) * HALF] = (sr * ei - si * er).astype(BF)

    def is_home(n):
        return jnp.logical_and(home == t, x == n)

    def give(src, dst, ss, rs, n):
        where = dst.at[slot, :, pl.ds(pl.multiple_of(c * HALF, HALF), HALF), :]

        @pl.when(is_home(n))
        def _():
            pltpu.make_async_copy(src.at[n], where, rs.at[slot, c]).start()

        @pl.when(jnp.logical_not(is_home(n)))
        def _():
            remote(src.at[n], where, ss.at[n], rs.at[slot, c], home, n).start()

    def give_wait(src, dst, ss, rs, n):
        where = dst.at[slot, :, pl.ds(pl.multiple_of(c * HALF, HALF), HALF), :]

        @pl.when(jnp.logical_not(is_home(n)))
        def _():
            remote(src.at[n], where, ss.at[n], rs.at[slot, c], home, n).wait_send()

    for h in range(2):
        for part in range(2):
            at = part * P_SIZE + h * HALF
            back2 = dot(gw[...], aq[:, at:at + HALF]).astype(BF)
            for n in range(2):
                b2s[2 * h + n, part] = back2[:, n * BLK:(n + 1) * BLK]
        for n in range(2):
            give(b2s, b2r, b2_ss, b2_rs, 2 * h + n)
    for n in range(4):
        give(t2s, t2r, t2_ss, t2_rs, n)

    for s in range(2):
        for r in range(2):
            receive(b2r.at[s, :, pl.ds(r * HALF, HALF), :], b2_rs.at[s, r])
    right = jnp.concatenate([
        jnp.concatenate([b2r[0, part], b2r[1, part]], axis=1) for part in range(2)], axis=0)
    for r in range(2):
        nr = dot(bq[r * HALF:(r + 1) * HALF, :], right)
        ni = dot(bq[P_SIZE + r * HALF:P_SIZE + (r + 1) * HALF, :], right)
        pr = probe[0, r * HALF:(r + 1) * HALF, :].astype(F32)
        pi = probe[1, r * HALF:(r + 1) * HALF, :].astype(F32)
        for s in range(2):
            sr, si = nr[:, s * BLK:(s + 1) * BLK], ni[:, s * BLK:(s + 1) * BLK]
            rows = slice(s * P_SIZE + r * HALF, s * P_SIZE + (r + 1) * HALF)
            tp[rows, :BLK] = (pr * sr + pi * si).astype(BF)
            tp[rows, BLK:] = (pr * si - pi * sr).astype(BF)

    def collect(which, terms):
        for first, last in ((1, 5), (5, 9), (0, 1)):
            total = dot(put[first * TH:last * TH, :], terms)
            if first == 0:
                for part in range(2):
                    out_ref[which, part] = total[:, part * BLK:(part + 1) * BLK]
                continue
            for k in range(first, last):
                outs[which, k] = total[(k - first) * TH:(k - first + 1) * TH].astype(BF)
                copy = remote(
                    outs.at[which, k], oin.at[which, k], out_ss.at[which, k],
                    out_rs.at[which, k], lax.rem(t + k, tiles), x,
                )
                copy.start()
                sends.append(copy)

    collect(0, tp[...])
    for s in range(2):
        for r in range(2):
            receive(t2r.at[s, :, pl.ds(r * HALF, HALF), :], t2_rs.at[s, r])
    terms = jnp.concatenate([
        jnp.concatenate([t2r[s, part] for part in range(2)], axis=1) for s in range(2)], axis=0)
    collect(1, terms)

    for which in range(2):
        for k in range(1, SPAN + 1):
            receive(oin.at[which, k], out_rs.at[which, k])
        for part in range(2):
            total = out_ref[which, part]
            for k in range(1, SPAN + 1):
                total = total + oin[which, k, :, part * BLK:(part + 1) * BLK].astype(F32)
            out_ref[which, part] = total

    for copy in sends:
        copy.wait_send()
    ex1.wait_send()
    ex2.wait_send()
    for s in range(2):
        for r in range(2):
            spread_wait(*amp_of(s, r))
            spread_wait(*h1_of(s, r))
            spread_wait(*o2_of(s, r))
    for n in range(4):
        give_wait(b2s, b2r, b2_ss, b2_rs, n)
        give_wait(t2s, t2r, t2_ss, t2_rs, n)


def shards(tiles, far, near, object_slab, probe_wave, amplitudes, row_offsets, position_counts):
    dma = pltpu.SemaphoreType.DMA
    vmem = pltpu.VMEM
    n2 = 2 * P_SIZE
    scratch = [
        vmem((2, 2, TH, BLK), F32),
        vmem((2, P_SIZE, BLK), BF),
        vmem((2, BLK, P_SIZE), F32),
        vmem((n2, n2), BF), vmem((n2, n2), BF), vmem((n2, n2), BF), vmem((n2, n2), BF),
        vmem((2, TH, HALF), BF),
        vmem((2, SPAN + 1, TH, HALF), BF),
        vmem((2, P_SIZE, P_SIZE + TH), BF),
        vmem((P_SIZE + TH, n2), BF),
        vmem((2, 2, P_SIZE, BLK), BF),
        vmem((2, 2, P_SIZE, BLK), BF),
        vmem((2, 2, BLK, HALF), BF),
        vmem((4, 2, HALF, BLK), BF),
        vmem((4, 2, HALF, BLK), BF),
        vmem((4, BLK, HALF), BF),
        vmem((2, 2, HALF, HALF), BF),
        vmem((HALF, n2), BF),
        vmem((2, HALF, HALF), BF),
        vmem((2, 2, HALF, HALF), BF),
        vmem((n2, HALF), BF),
        vmem((2, HALF, HALF), BF),
        vmem((2, 2, HALF, HALF), BF),
        vmem((4, 2, HALF, BLK), BF),
        vmem((HALF, n2), BF),
        vmem((4, 2, HALF, BLK), BF),
        vmem((2, 2, P_SIZE, BLK), BF),
        vmem((2, 2, P_SIZE, BLK), BF),
        vmem((n2, HALF), BF),
        vmem((2, SPAN + 1, TH, HALF), BF),
        vmem((2, SPAN + 1, TH, HALF), BF),
        dma((3,)), dma((4, 3)),
        dma((2, SPAN + 1)), dma((2, SPAN + 1)),
        dma((2, 2)), dma((4,)), dma((2, 2)), dma((4,)), dma((2, 2)), dma((4,)),
        dma, dma, dma, dma,
        dma((4,)), dma((2, 2)), dma((4,)), dma((2, 2)),
        dma((2, SPAN + 1)), dma((2, SPAN + 1)),
    ]
    any_spec = pl.BlockSpec(memory_space=pl.ANY)
    smem_spec = pl.BlockSpec(memory_space=pltpu.SMEM)
    return pl.pallas_call(
        functools.partial(body, tiles),
        out_shape=jax.ShapeDtypeStruct(object_slab.shape, F32),
        in_specs=[smem_spec, smem_spec] + [any_spec] * 5,
        out_specs=pl.BlockSpec(memory_space=pltpu.VMEM),
        scratch_shapes=scratch,
        compiler_params=pltpu.CompilerParams(
            collective_id=0, has_side_effects=True, vmem_limit_bytes=48 * 1024 * 1024
        ),
        name="object_gradient",
    )(row_offsets, position_counts, object_slab, probe_wave, amplitudes, near, far)


def solution(mesh):
    in_specs = (
        P(None, None, "tile", "scan"),
        P(None, None, "scan"),
        P("tile", "scan", None),
        P("tile"),
        P("tile"),
    )
    out_specs = P(None, None, "tile", "scan")
    far, near = tables()
    run = functools.partial(shards, mesh.shape["tile"], far, near)
    return jax.shard_map(run, mesh=mesh, in_specs=in_specs, out_specs=out_specs, check_vma=False)
```

profile of v0, /device:TPU:6, one launch (start us, length us, event | category | flops | bytes accessed | tf_op | source)
XLA Modules:
  0.0 69.0 jit_solution(9054480287458568511)
XLA Ops:
  0.0 0.0 copy-start.5
  0.7 0.0 copy-done.5
  0.7 0.0 copy-start
  0.7 1.2 %copy-done = bf16[2,512,512]{2,1,0:T(8,128)(2,1)S(1)} copy-done((bf16[2,512,512]{2,1,0:T(8,128)(2,1)S(1)}, bf16[2,512,512]{2,1,0:T(8,128)(2,1)}, u32[]{:S(2)}) %copy-start) | copy-done | bytes 1048600
  1.9 0.0 copy-start.1
  1.9 1.2 %copy-done.1 = bf16[2,512,512]{2,1,0:T(8,128)(2,1)S(1)} copy-done((bf16[2,512,512]{2,1,0:T(8,128)(2,1)S(1)}, bf16[2,512,512]{2,1,0:T(8,128)(2,1)}, u32[]{:S(2)}) %copy-start.1) | copy-done | bytes 1048600
  3.1 0.0 copy-start.2
  3.1 1.0 %copy-done.2 = f32[2,128,512]{2,1,0:T(8,128)S(1)} copy-done((f32[2,128,512]{2,1,0:T(8,128)S(1)}, f32[2,128,512]{2,1,0:T(8,128)}, u32[]{:S(2)}) %copy-start.2) | copy-done | bytes 524312
  4.2 0.0 copy-start.3
  4.2 0.9 %copy-done.3 = bf16[2,512,128]{2,1,0:T(8,128)(2,1)S(1)} copy-done((bf16[2,512,128]{2,1,0:T(8,128)(2,1)S(1)}, bf16[2,512,128]{2,1,0:T(8,128)(2,1)}, u32[]{:S(2)}) %copy-start.3) | copy-done | bytes 262168
  5.1 0.0 copy-start.4
  5.1 0.9 %copy-done.4 = f32[2,2,64,128]{3,2,1,0:T(8,128)S(1)} copy-done((f32[2,2,64,128]{3,2,1,0:T(8,128)S(1)}, f32[2,2,64,128]{3,2,1,0:T(8,128)}, u32[]{:S(2)}) %copy-start.4) | copy-done | bytes 131096
  6.0 62.3 %object_gradient.1 = f32[2,2,64,128]{3,2,1,0:T(8,128)S(1)} custom-call(s32[2]{0:T(128)S(1)} %copy-done.5, s32[1]{0:T(128)S(6)} %copy.9.cnt_ref, f32[2,2,64,128]{3,2,1,0:T(8,128)S(1)} %copy-done.4, bf16[2,512,128]{2,1,0:T(8,128)(2,1)S(1)} %copy-done.3, f32[2,128,512]{2,1,0:T(8,128)S(1)} %copy-done.2, bf16[2,512,512]{2,1,0:T(8,128)(2,1)S(1)} %copy-done.1, ...), custom_call_target="tpu_custom_call" | custom-call | tf_op jit(solution)/shard_map/object_gradient/pallas_call | solution.py:418
  68.4 0.7 copy.10
Async XLA Ops:
  0.0 0.7 copy-start.5
  0.7 1.2 %copy-start = (bf16[2,512,512]{2,1,0:T(8,128)(2,1)S(1)}, bf16[2,512,512]{2,1,0:T(8,128)(2,1)}, u32[]{:S(2)}) copy-start(bf16[2,512,512]{2,1,0:T(8,128)(2,1)} %constant.5.clone.tf_hbm) | copy-start | bytes 3145732
  1.9 1.2 %copy-start.1 = (bf16[2,512,512]{2,1,0:T(8,128)(2,1)S(1)}, bf16[2,512,512]{2,1,0:T(8,128)(2,1)}, u32[]{:S(2)}) copy-start(bf16[2,512,512]{2,1,0:T(8,128)(2,1)} %constant.4.clone.tq_hbm) | copy-start | bytes 3145732
  3.1 1.0 %copy-start.2 = (f32[2,128,512]{2,1,0:T(8,128)S(1)}, f32[2,128,512]{2,1,0:T(8,128)}, u32[]{:S(2)}) copy-start(f32[2,128,512]{2,1,0:T(8,128)} %amp_hbm.1) | copy-start | bytes 1572868
  4.2 0.9 %copy-start.3 = (bf16[2,512,128]{2,1,0:T(8,128)(2,1)S(1)}, bf16[2,512,128]{2,1,0:T(8,128)(2,1)}, u32[]{:S(2)}) copy-start(bf16[2,512,128]{2,1,0:T(8,128)(2,1)} %probe_hbm.1) | copy-start | bytes 786436
  5.1 0.9 %copy-start.4 = (f32[2,2,64,128]{3,2,1,0:T(8,128)S(1)}, f32[2,2,64,128]{3,2,1,0:T(8,128)}, u32[]{:S(2)}) copy-start(f32[2,2,64,128]{3,2,1,0:T(8,128)} %slab_hbm.1) | copy-start | bytes 393220
where the time goes:
time: 69.3 us; the launch traced here: 69 us
  Pallas kernels  62.3 us (90%)
  local copies, waits for them, and re-layouts  6 us (9%)
  between operations  0.7 us (1%)
    pallas_call x1, Pallas kernels, shards(): pl.pallas_call(functools.partial(body, tiles), out_shape=jax.ShapeDtypeSt...  62.3 us
    unnamed x13, local copies, waits for them, and re-layouts  6 us

commit v1 on v0

--- a/solution.py
+++ b/solution.py
@@ -40,22 +40,22 @@
 
 def body(
     tiles,
-    off_ref, cnt_ref, slab_hbm, probe_hbm, amp_hbm, tq_hbm, tf_hbm,
+    off_hbm, cnt_hbm, slab_hbm, probe_hbm, amp_hbm, tq_hbm, tf_hbm,
     out_ref,
-    slab, probe, ampf, aq, bq, af, bf,
-    stage, win, sel, put, h1, o2p, ampb, hr, o2r, amp,
-    ps, ew, gs, x1, ch, ks, y, t2s, gw, b2s, b2r, t2r, tp, outs, oin,
+    off_ref, cnt_ref, slab, probe, ampf, aq, bq, af, bf,
+    win, sel, put, h1, o2p, ampb, hr, o2r, amp,
+    ps, ew, gs, x1, ch, ks, y, t2s, gw, b2s, b2r, t2r, tp, odd, got, even, outs, oin,
     loc_sem, tab_sem,
-    in_ss, in_rs, h1_ss, h1_rs, o2_ss, o2_rs, am_ss, am_rs,
-    e1_ss, e1_rs, e2_ss, e2_rs, b2_ss, b2_rs, t2_ss, t2_rs, out_ss, out_rs,
+    in_ss, in_rs, fw_ss, h1_ss, h1_rs, o2_ss, o2_rs, am_ss, am_rs,
+    e1_ss, e1_rs, e2_ss, e2_rs, b2_ss, b2_rs, t2_ss, t2_rs, od_ss, od_rs, out_ss, out_rs,
 ):
     t = lax.axis_index("tile")
     x = lax.axis_index("scan")
     c = lax.rem(t, 2)
     d = 1 - c
     pair = t - c
-    home = pair + x // 2
-    slot = lax.rem(x, 2)
+    home = pair + lax.rem(x, 2)
+    slot = x // 2
 
     def remote(src, dst, ss, rs, tile, scan):
         return pltpu.make_async_remote_copy(
@@ -63,6 +63,16 @@
             device_id={"tile": tile, "scan": scan}, device_id_type=MESH,
         )
 
+    loads = [
+        pltpu.make_async_copy(slab_hbm, slab, loc_sem.at[0]),
+        pltpu.make_async_copy(amp_hbm, ampf, loc_sem.at[1]),
+        pltpu.make_async_copy(probe_hbm, probe, loc_sem.at[2]),
+        pltpu.make_async_copy(off_hbm, off_ref, loc_sem.at[3]),
+        pltpu.make_async_copy(cnt_hbm, cnt_ref, loc_sem.at[4]),
+    ]
+    for load in loads:
+        load.start()
+
     barrier = pltpu.get_barrier_semaphore()
 
     def greet(tile, scan):
@@ -70,20 +80,13 @@
             barrier, inc=1, device_id={"tile": tile, "scan": scan}, device_id_type=MESH
         )
 
-    for k in range(1, SPAN + 1):
+    greet(pair + d, x)
+    for k in range(2, SPAN + 1, 2):
         greet(lax.rem(t + k, tiles), x)
         greet(lax.rem(t + tiles - k, tiles), x)
     for step in range(1, 4):
         for core in range(2):
             greet(pair + core, lax.rem(x + step, 4))
-
-    loads = [
-        pltpu.make_async_copy(slab_hbm, slab, loc_sem.at[0]),
-        pltpu.make_async_copy(amp_hbm, ampf, loc_sem.at[1]),
-        pltpu.make_async_copy(probe_hbm, probe, loc_sem.at[2]),
-    ]
-    for load in loads:
-        load.start()
 
     def table_loads(src, dst, which, column):
         copies = []
@@ -108,39 +111,47 @@
     loads[0].wait()
     for s in range(2):
         for part in range(2):
-            piece = slab[s, part].astype(BF)
-            stage[s, :, part * BLK:(part + 1) * BLK] = piece
-            win[s, 0, :, part * BLK:(part + 1) * BLK] = piece
-    loads[1].wait()
-    for s in range(2):
-        for r in range(2):
-            ampb[s, r] = ampf[s, :, r * HALF:(r + 1) * HALF].astype(BF)
+            win[s, 0, :, part * BLK:(part + 1) * BLK] = slab[s, part].astype(BF)
+
+    pl.semaphore_wait(barrier, SPAN + 7)
+
+    sends = []
+
+    def start(copy):
+        copy.start()
+        sends.append(copy)
+
+    for s in range(2):
+        for k in range(2, SPAN + 1, 2):
+            start(remote(
+                win.at[s, 0], win.at[s, k], in_ss.at[s, k // 2], in_rs.at[s, k],
+                lax.rem(t + tiles - k, tiles), x,
+            ))
+
+    def pass_on(s, m):
+        k = 2 * m - 1 + 2 * c
+        return remote(
+            win.at[s, 2 * m], win.at[s, k], fw_ss.at[s, m], in_rs.at[s, k], pair + d, x)
+
+    for s in range(2):
+        @pl.when(c == 1)
+        def _():
+            pass_on(s, 0).start()
+
+    loads[3].wait()
+    loads[4].wait()
     for s in range(2):
         shape = (P_SIZE, P_SIZE + TH)
         shifted = lax.broadcasted_iota(jnp.int32, shape, 0) + off_ref[s]
         match = shifted == lax.broadcasted_iota(jnp.int32, shape, 1)
         sel[s] = jnp.where(match, 1.0, 0.0).astype(BF)
-        shape = (P_SIZE + TH, P_SIZE)
-        shifted = lax.broadcasted_iota(jnp.int32, shape, 1) + off_ref[s]
-        match = shifted == lax.broadcasted_iota(jnp.int32, shape, 0)
-        alive = jnp.broadcast_to(cnt_ref[0], shape) > s
-        put[:, s * P_SIZE:(s + 1) * P_SIZE] = jnp.where(
-            jnp.logical_and(match, alive), 1.0, 0.0).astype(BF)
-
-    pl.semaphore_wait(barrier, 2 * SPAN + 6)
-
-    sends = []
-    for s in range(2):
-        for k in range(1, SPAN + 1):
-            copy = remote(
-                stage.at[s], win.at[s, k], in_ss.at[s, k], in_rs.at[s, k],
-                lax.rem(t + tiles - k, tiles), x,
-            )
-            copy.start()
-            sends.append(copy)
+    loads[1].wait()
+    for s in range(2):
+        for r in range(2):
+            ampb[s, r] = ampf[s, :, r * HALF:(r + 1) * HALF].astype(BF)
 
     def is_self(s, r):
-        return jnp.logical_and(2 * c + s == x, c == r)
+        return jnp.logical_and(2 * s + c == x, c == r)
 
     def spread(src, dst, ss, rs, s, r):
         mine = is_self(s, r)
@@ -151,12 +162,12 @@
 
         @pl.when(jnp.logical_not(mine))
         def _():
-            remote(src, dst.at[x], ss.at[s, r], rs.at[x], pair + r, 2 * c + s).start()
+            remote(src, dst.at[x], ss.at[s, r], rs.at[x], pair + r, 2 * s + c).start()
 
     def spread_wait(src, dst, ss, rs, s, r):
         @pl.when(jnp.logical_not(is_self(s, r)))
         def _():
-            remote(src, dst.at[x], ss.at[s, r], rs.at[x], pair + r, 2 * c + s).wait_send()
+            remote(src, dst.at[x], ss.at[s, r], rs.at[x], pair + r, 2 * s + c).wait_send()
 
     def amp_of(s, r):
         return ampb.at[s, r], amp, am_ss, am_rs, s, r
@@ -180,7 +191,13 @@
         pltpu.make_async_copy(dst, dst, rs).wait()
 
     def window(s):
-        for k in range(1, SPAN + 1):
+        for m in range(1, 5):
+            receive(win.at[s, 2 * m], in_rs.at[s, 2 * m])
+
+            @pl.when(jnp.logical_or(c == 0, m < 4))
+            def _():
+                pass_on(s, m).start()
+        for k in range(1, SPAN + 1, 2):
             receive(win.at[s, k], in_rs.at[s, k])
         return jnp.concatenate([win[s, k] for k in range(SPAN + 1)], axis=0)
 
@@ -206,6 +223,14 @@
         for s in range(2):
             spread(*h1_of(s, r))
 
+    for s in range(2):
+        for b, k in enumerate((1, 3, 5, 7, 2, 4, 6, 8, 0)):
+            shape = (TH, P_SIZE)
+            shifted = lax.broadcasted_iota(jnp.int32, shape, 1) + off_ref[s]
+            match = shifted == lax.broadcasted_iota(jnp.int32, shape, 0) + k * TH
+            alive = jnp.broadcast_to(cnt_ref[0], shape) > s
+            put[b * TH:(b + 1) * TH, s * P_SIZE:(s + 1) * P_SIZE] = jnp.where(
+                jnp.logical_and(match, alive), 1.0, 0.0).astype(BF)
     wide = window(1)
     for s in range(2):
         patch = dot(sel[s], wide).astype(BF)
@@ -326,40 +351,52 @@
             tp[rows, BLK:] = (pr * si - pi * sr).astype(BF)
 
     def collect(which, terms):
-        for first, last in ((1, 5), (5, 9), (0, 1)):
-            total = dot(put[first * TH:last * TH, :], terms)
-            if first == 0:
-                for part in range(2):
-                    out_ref[which, part] = total[:, part * BLK:(part + 1) * BLK]
-                continue
-            for k in range(first, last):
-                outs[which, k] = total[(k - first) * TH:(k - first + 1) * TH].astype(BF)
-                copy = remote(
-                    outs.at[which, k], oin.at[which, k], out_ss.at[which, k],
-                    out_rs.at[which, k], lax.rem(t + k, tiles), x,
-                )
-                copy.start()
-                sends.append(copy)
+        total = dot(put[:HALF, :], terms)
+        for m in range(4):
+            odd[which, m] = total[m * TH:(m + 1) * TH].astype(BF)
+            start(remote(
+                odd.at[which, m], got.at[which, m], od_ss.at[which, m], od_rs.at[which, m],
+                pair + d, x))
+        total = dot(put[HALF:, :], terms)
+        for m in range(1, 5):
+            even[which, m] = total[(m - 1) * TH:m * TH]
+        even[which, 0] = total[HALF:]
+
+    def hand_on(which):
+        for m in range(4):
+            receive(got.at[which, m], od_rs.at[which, m])
+            even[which, m + d] += got[which, m].astype(F32)
+        for m in range(1, 5):
+            outs[which, m] = even[which, m].astype(BF)
+            start(remote(
+                outs.at[which, m], oin.at[which, m], out_ss.at[which, m],
+                out_rs.at[which, m], lax.rem(t + 2 * m, tiles), x))
 
     collect(0, tp[...])
+    hand_on(0)
     for s in range(2):
         for r in range(2):
             receive(t2r.at[s, :, pl.ds(r * HALF, HALF), :], t2_rs.at[s, r])
     terms = jnp.concatenate([
         jnp.concatenate([t2r[s, part] for part in range(2)], axis=1) for s in range(2)], axis=0)
     collect(1, terms)
+    hand_on(1)
 
     for which in range(2):
-        for k in range(1, SPAN + 1):
-            receive(oin.at[which, k], out_rs.at[which, k])
+        total = even[which, 0]
+        for m in range(1, 5):
+            receive(oin.at[which, m], out_rs.at[which, m])
+            total = total + oin[which, m].astype(F32)
         for part in range(2):
-            total = out_ref[which, part]
-            for k in range(1, SPAN + 1):
-                total = total + oin[which, k, :, part * BLK:(part + 1) * BLK].astype(F32)
-            out_ref[which, part] = total
+            out_ref[which, part] = total[:, part * BLK:(part + 1) * BLK]
 
     for copy in sends:
         copy.wait_send()
+    for s in range(2):
+        for m in range(5):
+            @pl.when(jnp.logical_and(m < 4, c == 1) if m == 0 else jnp.logical_or(c == 0, m < 4))
+            def _():
+                pass_on(s, m).wait_send()
     ex1.wait_send()
     ex2.wait_send()
     for s in range(2):
@@ -377,11 +414,11 @@
     vmem = pltpu.VMEM
     n2 = 2 * P_SIZE
     scratch = [
+        pltpu.SMEM((2,), jnp.int32), pltpu.SMEM((1,), jnp.int32),
         vmem((2, 2, TH, BLK), F32),
         vmem((2, P_SIZE, BLK), BF),
         vmem((2, BLK, P_SIZE), F32),
         vmem((n2, n2), BF), vmem((n2, n2), BF), vmem((n2, n2), BF), vmem((n2, n2), BF),
-        vmem((2, TH, HALF), BF),
         vmem((2, SPAN + 1, TH, HALF), BF),
         vmem((2, P_SIZE, P_SIZE + TH), BF),
         vmem((P_SIZE + TH, n2), BF),
@@ -404,25 +441,27 @@
         vmem((2, 2, P_SIZE, BLK), BF),
         vmem((2, 2, P_SIZE, BLK), BF),
         vmem((n2, HALF), BF),
-        vmem((2, SPAN + 1, TH, HALF), BF),
-        vmem((2, SPAN + 1, TH, HALF), BF),
-        dma((3,)), dma((4, 3)),
-        dma((2, SPAN + 1)), dma((2, SPAN + 1)),
+        vmem((2, 4, TH, HALF), BF),
+        vmem((2, 4, TH, HALF), BF),
+        vmem((2, 5, TH, HALF), F32),
+        vmem((2, 5, TH, HALF), BF),
+        vmem((2, 5, TH, HALF), BF),
+        dma((5,)), dma((4, 3)),
+        dma((2, 5)), dma((2, SPAN + 1)), dma((2, 5)),
         dma((2, 2)), dma((4,)), dma((2, 2)), dma((4,)), dma((2, 2)), dma((4,)),
         dma, dma, dma, dma,
         dma((4,)), dma((2, 2)), dma((4,)), dma((2, 2)),
-        dma((2, SPAN + 1)), dma((2, SPAN + 1)),
+        dma((2, 4)), dma((2, 4)), dma((2, 5)), dma((2, 5)),
     ]
     any_spec = pl.BlockSpec(memory_space=pl.ANY)
-    smem_spec = pl.BlockSpec(memory_space=pltpu.SMEM)
     return pl.pallas_call(
         functools.partial(body, tiles),
         out_shape=jax.ShapeDtypeStruct(object_slab.shape, F32),
-        in_specs=[smem_spec, smem_spec] + [any_spec] * 5,
+        in_specs=[any_spec] * 7,
         out_specs=pl.BlockSpec(memory_space=pltpu.VMEM),
         scratch_shapes=scratch,
         compiler_params=pltpu.CompilerParams(
-            collective_id=0, has_side_effects=True, vmem_limit_bytes=48 * 1024 * 1024
+            collective_id=0, has_side_effects=True, vmem_limit_bytes=67_000_000
         ),
         name="object_gradient",
     )(row_offsets, position_counts, object_slab, probe_wave, amplitudes, near, far)

time: 69.3 us -> 63.8 us (0.921)
  local copies, waits for them, and re-layouts: 6 us -> 1.57 us
  Pallas kernels: 62.3 us -> 61.4 us
    unnamed x13 -> x1, local copies, waits for them, and re-layouts: 6 us -> 1.57 us
    pallas_call x1, Pallas kernels: 62.3 us -> 61.4 us  [shards(): pl.pallas_call(functools.partial(body, tiles), out_shape=jax.ShapeDtypeSt...]
where the time goes in v1:
time: 63.8 us; the launch traced here: 63.6 us
  Pallas kernels  61.4 us (96%)
  local copies, waits for them, and re-layouts  1.57 us (2%)
  between operations  0.66 us (1%)
    pallas_call x1, Pallas kernels, shards(): pl.pallas_call(functools.partial(body, tiles), out_shape=jax.ShapeDtypeSt...  61.4 us
    unnamed x1, local copies, waits for them, and re-layouts  1.57 us

profile of v1, /device:TPU:6, one launch (start us, length us, event | category | flops | bytes accessed | tf_op | source)
XLA Modules:
  0.0 63.6 jit_solution(492094577840353866)
XLA Ops:
  0.7 61.4 %object_gradient.1 = f32[2,2,64,128]{3,2,1,0:T(8,128)} custom-call(s32[2]{0:T(128)} %off_hbm.1, s32[1]{0:T(128)S(6)} %copy.9.cnt_hbm, f32[2,2,64,128]{3,2,1,0:T(8,128)} %slab_hbm.1, bf16[2,512,128]{2,1,0:T(8,128)(2,1)} %probe_hbm.1, f32[2,128,512]{2,1,0:T(8,128)} %amp_hbm.1, bf16[2,512,512]{2,1,0:T(8,128)(2,1)} %constant.4.clone.tq_hbm, ...), custom_call_target="tpu_custom_call" | custom-call | tf_op jit(solution)/shard_map/object_gradient/pallas_call | solution.py:457
  62.0 1.6 %copy.10 = f32[2,2,64,128]{3,2,1,0:T(8,128)} copy(f32[2,2,64,128]{3,2,1,0:T(8,128)} %object_gradient.1) | data formatting | bytes 262144

commit v2 on v1

--- a/solution.py
+++ b/solution.py
@@ -43,10 +43,11 @@
     off_hbm, cnt_hbm, slab_hbm, probe_hbm, amp_hbm, tq_hbm, tf_hbm,
     out_ref,
     off_ref, cnt_ref, slab, probe, ampf, aq, bq, af, bf,
-    win, sel, put, h1, o2p, ampb, hr, o2r, amp,
+    win, o2g, o2w, offb, sel, psel, put, h1, ampb, hr, o2r, amp,
     ps, ew, gs, x1, ch, ks, y, t2s, gw, b2s, b2r, t2r, tp, odd, got, even, outs, oin,
     loc_sem, tab_sem,
-    in_ss, in_rs, fw_ss, h1_ss, h1_rs, o2_ss, o2_rs, am_ss, am_rs,
+    in_ss, in_rs, fw_ss, og_ss, og_rs, up_ss, up_rs, of_ss, of_rs,
+    h1_ss, h1_rs, o2_ss, o2_rs, am_ss, am_rs,
     e1_ss, e1_rs, e2_ss, e2_rs, b2_ss, b2_rs, t2_ss, t2_rs, od_ss, od_rs, out_ss, out_rs,
 ):
     t = lax.axis_index("tile")
@@ -56,6 +57,9 @@
     pair = t - c
     home = pair + lax.rem(x, 2)
     slot = x // 2
+    odd_home = lax.rem(x, 2)
+    row = lax.rem(t // 2, 4)
+    plane = t - lax.rem(t, 8)
 
     def remote(src, dst, ss, rs, tile, scan):
         return pltpu.make_async_remote_copy(
@@ -80,7 +84,8 @@
             barrier, inc=1, device_id={"tile": tile, "scan": scan}, device_id_type=MESH
         )
 
-    greet(pair + d, x)
+    for n in range(1, 8):
+        greet(plane + lax.rem(t + n, 8), x)
     for k in range(2, SPAN + 1, 2):
         greet(lax.rem(t + k, tiles), x)
         greet(lax.rem(t + tiles - k, tiles), x)
@@ -109,11 +114,17 @@
     af_loads = table_loads(tf_hbm, af, 3, 0)
 
     loads[0].wait()
-    for s in range(2):
-        for part in range(2):
-            win[s, 0, :, part * BLK:(part + 1) * BLK] = slab[s, part].astype(BF)
-
-    pl.semaphore_wait(barrier, SPAN + 7)
+    for part in range(2):
+        win[0, :, part * BLK:(part + 1) * BLK] = slab[0, part].astype(BF)
+        o2g[0, x, :, part * BLK:(part + 1) * BLK] = slab[1, part].astype(BF)
+    loads[3].wait()
+    loads[4].wait()
+    shape = (8, 3 * BLK)
+    offset = jnp.broadcast_to(off_ref[slot], shape)
+    alive = jnp.broadcast_to(cnt_ref[0], shape) > jnp.broadcast_to(slot, shape)
+    offb[c] = jnp.where(alive, offset, -2 * P_SIZE).astype(F32)
+
+    pl.semaphore_wait(barrier, SPAN + 13)
 
     sends = []
 
@@ -121,25 +132,24 @@
         copy.start()
         sends.append(copy)
 
-    for s in range(2):
-        for k in range(2, SPAN + 1, 2):
-            start(remote(
-                win.at[s, 0], win.at[s, k], in_ss.at[s, k // 2], in_rs.at[s, k],
-                lax.rem(t + tiles - k, tiles), x,
-            ))
-
-    def pass_on(s, m):
+    for k in range(2, SPAN + 1, 2):
+        start(remote(
+            win.at[0], win.at[k], in_ss.at[k // 2], in_rs.at[k], lax.rem(t + tiles - k, tiles), x))
+
+    def pass_on(m):
         k = 2 * m - 1 + 2 * c
-        return remote(
-            win.at[s, 2 * m], win.at[s, k], fw_ss.at[s, m], in_rs.at[s, k], pair + d, x)
-
-    for s in range(2):
-        @pl.when(c == 1)
-        def _():
-            pass_on(s, 0).start()
-
-    loads[3].wait()
-    loads[4].wait()
+        return remote(win.at[2 * m], win.at[k], fw_ss.at[m], in_rs.at[k], pair + d, x)
+
+    @pl.when(c == 1)
+    def _():
+        pass_on(0).start()
+
+    for step in range(1, 4):
+        start(remote(
+            o2g.at[0, x], o2g.at[0, x], og_ss.at[step - 1], og_rs.at[x],
+            t, lax.rem(x + step, 4)))
+    start(remote(offb.at[c], offb.at[c], of_ss, of_rs, pair + d, x))
+
     for s in range(2):
         shape = (P_SIZE, P_SIZE + TH)
         shifted = lax.broadcasted_iota(jnp.int32, shape, 0) + off_ref[s]
@@ -175,9 +185,6 @@
     def h1_of(s, r):
         return h1.at[s, :, pl.ds(r * HALF, HALF), :], hr, h1_ss, h1_rs, s, r
 
-    def o2_of(s, r):
-        return o2p.at[s, :, pl.ds(r * HALF, HALF), :], o2r, o2_ss, o2_rs, s, r
-
     for s in range(2):
         for r in range(2):
             spread(*amp_of(s, r))
@@ -190,22 +197,64 @@
     def receive(dst, rs):
         pltpu.make_async_copy(dst, dst, rs).wait()
 
-    def window(s):
+    def plane_send(m, r, go, local):
+        place = 2 * m + c - odd_home - 4 * r
+        wanted = jnp.logical_and(place >= 0, place <= 4)
+        for source in range(2):
+            if m in (0, 4):
+                if source != m // 4:
+                    continue
+                tile, here = pair + r, wanted
+            else:
+                tile = plane + 2 * lax.rem(row - m + 4, 4) + r
+                here = jnp.logical_and(wanted, (m <= row) if source == 0 else (m > row))
+
+            def copy():
+                return remote(
+                    o2g.at[source], o2w.at[place], o2_ss.at[m, r], o2_rs.at[place], tile, x)
+
+            def own():
+                return pltpu.make_async_copy(o2g.at[source], o2w.at[place], o2_rs.at[place])
+
+            if source in go:
+                if m in (0, 4):
+                    @pl.when(jnp.logical_and(here, c != r))
+                    def _():
+                        copy().start() if local else copy().wait_send()
+
+                    if local:
+                        @pl.when(jnp.logical_and(here, c == r))
+                        def _():
+                            own().start()
+                else:
+                    @pl.when(here)
+                    def _():
+                        copy().start() if local else copy().wait_send()
+
+    for step in range(1, 4):
+        other = lax.rem(x + step, 4)
+        receive(o2g.at[0, other], og_rs.at[other])
+    start(remote(o2g.at[0], o2g.at[1], up_ss, up_rs, lax.rem(t + tiles - 8, tiles), x))
+    for m in range(4):
+        for r in range(2):
+            plane_send(m, r, (0,), True)
+
+    def window():
         for m in range(1, 5):
-            receive(win.at[s, 2 * m], in_rs.at[s, 2 * m])
+            receive(win.at[2 * m], in_rs.at[2 * m])
 
             @pl.when(jnp.logical_or(c == 0, m < 4))
             def _():
-                pass_on(s, m).start()
+                pass_on(m).start()
         for k in range(1, SPAN + 1, 2):
-            receive(win.at[s, k], in_rs.at[s, k])
-        return jnp.concatenate([win[s, k] for k in range(SPAN + 1)], axis=0)
+            receive(win.at[k], in_rs.at[k])
+        return jnp.concatenate([win[k] for k in range(SPAN + 1)], axis=0)
 
     def dot(left, right):
         return jnp.dot(left, right, preferred_element_type=F32)
 
     loads[2].wait()
-    wide = window(0)
+    wide = window()
     psi = []
     for s in range(2):
         patch = dot(sel[s], wide)
@@ -223,6 +272,11 @@
         for s in range(2):
             spread(*h1_of(s, r))
 
+    receive(o2g.at[1], up_rs)
+    for m in range(1, 5):
+        for r in range(2):
+            plane_send(m, r, (1,), True)
+
     for s in range(2):
         for b, k in enumerate((1, 3, 5, 7, 2, 4, 6, 8, 0)):
             shape = (TH, P_SIZE)
@@ -231,13 +285,11 @@
             alive = jnp.broadcast_to(cnt_ref[0], shape) > s
             put[b * TH:(b + 1) * TH, s * P_SIZE:(s + 1) * P_SIZE] = jnp.where(
                 jnp.logical_and(match, alive), 1.0, 0.0).astype(BF)
-    wide = window(1)
-    for s in range(2):
-        patch = dot(sel[s], wide).astype(BF)
-        for part in range(2):
-            o2p[s, part] = patch[:, part * BLK:(part + 1) * BLK]
-        for r in range(2):
-            spread(*o2_of(s, r))
+    receive(offb.at[d], of_rs)
+    shape = (HALF, HALF + TH)
+    shifted = lax.broadcasted_iota(jnp.int32, shape, 0).astype(F32) + offb[odd_home][0:1, :HALF + TH]
+    match = shifted == lax.broadcasted_iota(jnp.int32, shape, 1).astype(F32)
+    psel[...] = jnp.where(match, 1.0, 0.0).astype(BF)
 
     for n in range(4):
         receive(hr.at[n], h1_rs.at[n])
@@ -246,11 +298,15 @@
         for h in range(2):
             at = part * P_SIZE + h * HALF
             ps[part, h] = dot(left, bq[:, at:at + HALF]).astype(BF)
+    for k in range(5):
+        receive(o2w.at[k], o2_rs.at[k])
     for n in range(4):
-        receive(o2r.at[n], o2_rs.at[n])
+        rows = jnp.concatenate([o2w[k, n] for k in range(5)], axis=0)
+        o2r[n] = dot(psel[...], rows).astype(BF)
 
     def second(part, h):
-        return jnp.concatenate([o2r[2 * h, part], o2r[2 * h + 1, part]], axis=1).astype(F32)
+        columns = slice(part * BLK, (part + 1) * BLK)
+        return jnp.concatenate([o2r[2 * h, :, columns], o2r[2 * h + 1, :, columns]], axis=1).astype(F32)
 
     for h in range(2):
         wr, wi = ps[0, h].astype(F32), ps[1, h].astype(F32)
@@ -392,18 +448,18 @@
 
     for copy in sends:
         copy.wait_send()
-    for s in range(2):
-        for m in range(5):
-            @pl.when(jnp.logical_and(m < 4, c == 1) if m == 0 else jnp.logical_or(c == 0, m < 4))
-            def _():
-                pass_on(s, m).wait_send()
+    for m in range(5):
+        @pl.when((c == 1) if m == 0 else jnp.logical_or(c == 0, m < 4))
+        def _():
+            pass_on(m).wait_send()
+        for r in range(2):
+            plane_send(m, r, (0, 1), False)
     ex1.wait_send()
     ex2.wait_send()
     for s in range(2):
         for r in range(2):
             spread_wait(*amp_of(s, r))
             spread_wait(*h1_of(s, r))
-            spread_wait(*o2_of(s, r))
     for n in range(4):
         give_wait(b2s, b2r, b2_ss, b2_rs, n)
         give_wait(t2s, t2r, t2_ss, t2_rs, n)
@@ -419,14 +475,17 @@
         vmem((2, P_SIZE, BLK), BF),
         vmem((2, BLK, P_SIZE), F32),
         vmem((n2, n2), BF), vmem((n2, n2), BF), vmem((n2, n2), BF), vmem((n2, n2), BF),
-        vmem((2, SPAN + 1, TH, HALF), BF),
+        vmem((SPAN + 1, TH, HALF), BF),
+        vmem((2, 4, TH, HALF), BF),
+        vmem((5, 4, TH, HALF), BF),
+        vmem((2, 8, 3 * BLK), F32),
         vmem((2, P_SIZE, P_SIZE + TH), BF),
+        vmem((HALF, HALF + TH), BF),
         vmem((P_SIZE + TH, n2), BF),
-        vmem((2, 2, P_SIZE, BLK), BF),
         vmem((2, 2, P_SIZE, BLK), BF),
         vmem((2, 2, BLK, HALF), BF),
         vmem((4, 2, HALF, BLK), BF),
-        vmem((4, 2, HALF, BLK), BF),
+        vmem((4, HALF, HALF), BF),
         vmem((4, BLK, HALF), BF),
         vmem((2, 2, HALF, HALF), BF),
         vmem((HALF, n2), BF),
@@ -447,8 +506,8 @@
         vmem((2, 5, TH, HALF), BF),
         vmem((2, 5, TH, HALF), BF),
         dma((5,)), dma((4, 3)),
-        dma((2, 5)), dma((2, SPAN + 1)), dma((2, 5)),
-        dma((2, 2)), dma((4,)), dma((2, 2)), dma((4,)), dma((2, 2)), dma((4,)),
+        dma((5,)), dma((SPAN + 1,)), dma((5,)), dma((3,)), dma((4,)), dma, dma, dma, dma,
+        dma((2, 2)), dma((4,)), dma((5, 2)), dma((5,)), dma((2, 2)), dma((4,)),
         dma, dma, dma, dma,
         dma((4,)), dma((2, 2)), dma((4,)), dma((2, 2)),
         dma((2, 4)), dma((2, 4)), dma((2, 5)), dma((2, 5)),

time: 63.8 us -> 60.7 us (0.951); the launches traced: 63.6 us -> 59.6 us
  Pallas kernels: 61.4 us -> 57.4 us
    pallas_call x1, Pallas kernels: 61.4 us -> 57.4 us  [shards(): pl.pallas_call(functools.partial(body, tiles), out_shape=jax.ShapeDtypeSt...]
where the time goes in v2:
time: 60.7 us; the launch traced here: 59.6 us
  Pallas kernels  57.4 us (95%)
  local copies, waits for them, and re-layouts  1.57 us (3%)
  between operations  0.66 us (1%)
    pallas_call x1, Pallas kernels, shards(): pl.pallas_call(functools.partial(body, tiles), out_shape=jax.ShapeDtypeSt...  57.4 us
    unnamed x1, local copies, waits for them, and re-layouts  1.57 us

profile of v2, /device:TPU:6, one launch (start us, length us, event | category | flops | bytes accessed | tf_op | source)
XLA Modules:
  0.0 59.6 jit_solution(12346210917058390157)
XLA Ops:
  0.7 57.4 %object_gradient.1 = f32[2,2,64,128]{3,2,1,0:T(8,128)} custom-call(s32[2]{0:T(128)} %off_hbm.1, s32[1]{0:T(128)S(6)} %copy.9.cnt_hbm, f32[2,2,64,128]{3,2,1,0:T(8,128)} %slab_hbm.1, bf16[2,512,128]{2,1,0:T(8,128)(2,1)} %probe_hbm.1, f32[2,128,512]{2,1,0:T(8,128)} %amp_hbm.1, bf16[2,512,512]{2,1,0:T(8,128)(2,1)} %constant.4.clone.tq_hbm, ...), custom_call_target="tpu_custom_call" | custom-call | tf_op jit(solution)/shard_map/object_gradient/pallas_call | solution.py:516
  58.0 1.6 %copy.10 = f32[2,2,64,128]{3,2,1,0:T(8,128)} copy(f32[2,2,64,128]{3,2,1,0:T(8,128)} %object_gradient.1) | data formatting | bytes 262144

commit v3 on v2

--- a/solution.py
+++ b/solution.py
@@ -44,11 +44,12 @@
     out_ref,
     off_ref, cnt_ref, slab, probe, ampf, aq, bq, af, bf,
     win, o2g, o2w, offb, sel, psel, put, h1, ampb, hr, o2r, amp,
-    ps, ew, gs, x1, ch, ks, y, t2s, gw, b2s, b2r, t2r, tp, odd, got, even, outs, oin,
+    ps, ew, gs, x1, ch, ks, y, t2s, gw, b2s, b2r, tp, odd, got, even, outs, oin,
+    pput, t2o, rin, acc, uo, ui, xo, xi,
     loc_sem, tab_sem,
     in_ss, in_rs, fw_ss, og_ss, og_rs, up_ss, up_rs, of_ss, of_rs,
     h1_ss, h1_rs, o2_ss, o2_rs, am_ss, am_rs,
-    e1_ss, e1_rs, e2_ss, e2_rs, b2_ss, b2_rs, t2_ss, t2_rs, od_ss, od_rs, out_ss, out_rs,
+    e1_ss, e1_rs, e2_ss, e2_rs, b2_ss, b2_rs, rt_ss, rt_rs, uu_ss, uu_rs, xs_ss, xs_rs, od_ss, od_rs, out_ss, out_rs,
 ):
     t = lax.axis_index("tile")
     x = lax.axis_index("scan")
@@ -86,9 +87,20 @@
 
     for n in range(1, 8):
         greet(plane + lax.rem(t + n, 8), x)
+    def below(k):
+        return t - k >= 0
+
+    def above(k):
+        return t + k < tiles
+
     for k in range(2, SPAN + 1, 2):
-        greet(lax.rem(t + k, tiles), x)
-        greet(lax.rem(t + tiles - k, tiles), x)
+        @pl.when(above(k))
+        def _():
+            greet(t + k, x)
+
+        @pl.when(below(k))
+        def _():
+            greet(t - k, x)
     for step in range(1, 4):
         for core in range(2):
             greet(pair + core, lax.rem(x + step, 4))
@@ -124,17 +136,45 @@
     alive = jnp.broadcast_to(cnt_ref[0], shape) > jnp.broadcast_to(slot, shape)
     offb[c] = jnp.where(alive, offset, -2 * P_SIZE).astype(F32)
 
-    pl.semaphore_wait(barrier, SPAN + 13)
+    for m in range(1, 5):
+        @pl.when(jnp.logical_not(above(2 * m)))
+        def _():
+            win[2 * m] = jnp.zeros((TH, HALF), BF)
+
+        @pl.when(jnp.logical_not(below(2 * m)))
+        def _():
+            oin[0, m] = jnp.zeros((TH, HALF), BF)
+
+    @pl.when(jnp.logical_not(above(8)))
+    def _():
+        o2g[1] = jnp.zeros((4, TH, HALF), BF)
+
+    @pl.when(jnp.logical_not(below(8)))
+    def _():
+        ui[...] = jnp.zeros((4, TH, HALF), BF)
+
+    pl.semaphore_wait(
+        barrier, 13 + jnp.minimum(4, (tiles - 1 - t) // 2) + jnp.minimum(4, t // 2))
 
     sends = []
 
-    def start(copy):
-        copy.start()
-        sends.append(copy)
+    def start(copy, here=None):
+        sends.append((copy, here))
+        if here is None:
+            copy.start()
+        else:
+            pl.when(here)(copy.start)
+
+    def receive(dst, rs, here=None):
+        copy = pltpu.make_async_copy(dst, dst, rs)
+        if here is None:
+            copy.wait()
+        else:
+            pl.when(here)(copy.wait)
 
     for k in range(2, SPAN + 1, 2):
         start(remote(
-            win.at[0], win.at[k], in_ss.at[k // 2], in_rs.at[k], lax.rem(t + tiles - k, tiles), x))
+            win.at[0], win.at[k], in_ss.at[k // 2], in_rs.at[k], t - k, x), below(k))
 
     def pass_on(m):
         k = 2 * m - 1 + 2 * c
@@ -193,9 +233,6 @@
     table_ready(bq, bq_loads, 1)
     table_ready(bf, bf_loads, 1)
     table_ready(af, af_loads, 0)
-
-    def receive(dst, rs):
-        pltpu.make_async_copy(dst, dst, rs).wait()
 
     def plane_send(m, r, go, local):
         place = 2 * m + c - odd_home - 4 * r
@@ -234,14 +271,14 @@
     for step in range(1, 4):
         other = lax.rem(x + step, 4)
         receive(o2g.at[0, other], og_rs.at[other])
-    start(remote(o2g.at[0], o2g.at[1], up_ss, up_rs, lax.rem(t + tiles - 8, tiles), x))
+    start(remote(o2g.at[0], o2g.at[1], up_ss, up_rs, t - 8, x), below(8))
     for m in range(4):
         for r in range(2):
             plane_send(m, r, (0,), True)
 
     def window():
         for m in range(1, 5):
-            receive(win.at[2 * m], in_rs.at[2 * m])
+            receive(win.at[2 * m], in_rs.at[2 * m], above(2 * m))
 
             @pl.when(jnp.logical_or(c == 0, m < 4))
             def _():
@@ -272,7 +309,7 @@
         for s in range(2):
             spread(*h1_of(s, r))
 
-    receive(o2g.at[1], up_rs)
+    receive(o2g.at[1], up_rs, above(8))
     for m in range(1, 5):
         for r in range(2):
             plane_send(m, r, (1,), True)
@@ -290,6 +327,11 @@
     shifted = lax.broadcasted_iota(jnp.int32, shape, 0).astype(F32) + offb[odd_home][0:1, :HALF + TH]
     match = shifted == lax.broadcasted_iota(jnp.int32, shape, 1).astype(F32)
     psel[...] = jnp.where(match, 1.0, 0.0).astype(BF)
+    shape = (HALF + TH, HALF)
+    shifted = lax.broadcasted_iota(jnp.int32, shape, 1).astype(F32) + offb[odd_home][0:1, :HALF]
+    match = shifted == lax.broadcasted_iota(jnp.int32, shape, 0).astype(F32)
+    pput[...] = jnp.where(match, 1.0, 0.0).astype(BF)
+    acc[...] = jnp.zeros_like(acc)
 
     for n in range(4):
         receive(hr.at[n], h1_rs.at[n])
@@ -353,10 +395,46 @@
         sr, si = second(0, h), second(1, h)
         tr, ti = (wr * er + wi * ei).astype(BF), (wr * ei - wi * er).astype(BF)
         for n in range(2):
-            t2s[2 * h + n, 0] = tr[:, n * BLK:(n + 1) * BLK]
-            t2s[2 * h + n, 1] = ti[:, n * BLK:(n + 1) * BLK]
+            t2s[2 * h + n, :, :BLK] = tr[:, n * BLK:(n + 1) * BLK]
+            t2s[2 * h + n, :, BLK:] = ti[:, n * BLK:(n + 1) * BLK]
         gw[:, h * HALF:(h + 1) * HALF] = (sr * er + si * ei).astype(BF)
         gw[:, P_SIZE + h * HALF:P_SIZE + (h + 1) * HALF] = (sr * ei - si * er).astype(BF)
+
+    for n in range(4):
+        moved = dot(pput[...], t2s[n]).astype(BF)
+        for k in range(5):
+            t2o[k, n] = moved[k * TH:(k + 1) * TH]
+
+    def term_send(k, kind, begin):
+        place = k + odd_home + 4 * c
+        m = place // 2
+        core = lax.rem(place, 2)
+        tile = plane + 2 * lax.rem(row + m, 4) + core
+        copy = remote(t2o.at[k], rin.at[m, c], rt_ss.at[k], rt_rs.at[m, c], tile, x)
+        here = (row + m > 3) if kind else (row + m <= 3)
+
+        @pl.when(jnp.logical_and(here, tile != t))
+        def _():
+            copy.start() if begin else copy.wait_send()
+
+        if begin:
+            @pl.when(jnp.logical_and(here, tile == t))
+            def _():
+                pltpu.make_async_copy(t2o.at[k], rin.at[m, c], rt_rs.at[m, c]).start()
+
+    def term_take(m, r, kind):
+        place = 2 * m + c - odd_home - 4 * r
+        here = (m > row) if kind else (m <= row)
+
+        @pl.when(jnp.logical_and(here, jnp.logical_and(place >= 0, place <= 4)))
+        def _():
+            receive(rin.at[m, r], rt_rs.at[m, r])
+            acc[kind] += rin[m, r].astype(F32)
+
+    for k in reversed(range(5)):
+        term_send(k, 1, True)
+    for k in reversed(range(5)):
+        term_send(k, 0, True)
 
     def is_home(n):
         return jnp.logical_and(home == t, x == n)
@@ -387,8 +465,12 @@
                 b2s[2 * h + n, part] = back2[:, n * BLK:(n + 1) * BLK]
         for n in range(2):
             give(b2s, b2r, b2_ss, b2_rs, 2 * h + n)
-    for n in range(4):
-        give(t2s, t2r, t2_ss, t2_rs, n)
+
+    for m in reversed(range(1, 5)):
+        for r in range(2):
+            term_take(m, r, 1)
+    uo[...] = acc[1].astype(BF)
+    start(remote(uo, ui, uu_ss, uu_rs, t + 8, x), above(8))
 
     for s in range(2):
         for r in range(2):
@@ -426,34 +508,49 @@
             outs[which, m] = even[which, m].astype(BF)
             start(remote(
                 outs.at[which, m], oin.at[which, m], out_ss.at[which, m],
-                out_rs.at[which, m], lax.rem(t + 2 * m, tiles), x))
+                out_rs.at[which, m], t + 2 * m, x), above(2 * m))
 
     collect(0, tp[...])
     hand_on(0)
-    for s in range(2):
-        for r in range(2):
-            receive(t2r.at[s, :, pl.ds(r * HALF, HALF), :], t2_rs.at[s, r])
-    terms = jnp.concatenate([
-        jnp.concatenate([t2r[s, part] for part in range(2)], axis=1) for s in range(2)], axis=0)
-    collect(1, terms)
-    hand_on(1)
-
-    for which in range(2):
-        total = even[which, 0]
-        for m in range(1, 5):
-            receive(oin.at[which, m], out_rs.at[which, m])
-            total = total + oin[which, m].astype(F32)
-        for part in range(2):
-            out_ref[which, part] = total[:, part * BLK:(part + 1) * BLK]
-
-    for copy in sends:
-        copy.wait_send()
+    for m in range(4):
+        for r in range(2):
+            term_take(m, r, 0)
+    receive(ui, uu_rs, below(8))
+    acc[0] += ui[...].astype(F32)
+    xo[...] = acc[0].astype(BF)
+    for step in range(1, 4):
+        other = lax.rem(x + step, 4)
+        start(remote(xo.at[other], xi.at[x], xs_ss.at[step - 1], xs_rs.at[x], t, other))
+
+    total = even[0, 0]
+    for m in range(1, 5):
+        receive(oin.at[0, m], out_rs.at[0, m], below(2 * m))
+        total = total + oin[0, m].astype(F32)
+    for part in range(2):
+        out_ref[0, part] = total[:, part * BLK:(part + 1) * BLK]
+
+    total = acc[0, x]
+    for step in range(1, 4):
+        other = lax.rem(x + step, 4)
+        receive(xi.at[other], xs_rs.at[other])
+        total = total + xi[other].astype(F32)
+    for part in range(2):
+        out_ref[1, part] = total[:, part * BLK:(part + 1) * BLK]
+
+    for copy, here in sends:
+        if here is None:
+            copy.wait_send()
+        else:
+            pl.when(here)(copy.wait_send)
     for m in range(5):
         @pl.when((c == 1) if m == 0 else jnp.logical_or(c == 0, m < 4))
         def _():
             pass_on(m).wait_send()
         for r in range(2):
             plane_send(m, r, (0, 1), False)
+    for k in range(5):
+        term_send(k, 0, False)
+        term_send(k, 1, False)
     ex1.wait_send()
     ex2.wait_send()
     for s in range(2):
@@ -462,7 +559,6 @@
             spread_wait(*h1_of(s, r))
     for n in range(4):
         give_wait(b2s, b2r, b2_ss, b2_rs, n)
-        give_wait(t2s, t2r, t2_ss, t2_rs, n)
 
 
 def shards(tiles, far, near, object_slab, probe_wave, amplitudes, row_offsets, position_counts):
@@ -494,10 +590,9 @@
         vmem((n2, HALF), BF),
         vmem((2, HALF, HALF), BF),
         vmem((2, 2, HALF, HALF), BF),
-        vmem((4, 2, HALF, BLK), BF),
+        vmem((4, HALF, HALF), BF),
         vmem((HALF, n2), BF),
         vmem((4, 2, HALF, BLK), BF),
-        vmem((2, 2, P_SIZE, BLK), BF),
         vmem((2, 2, P_SIZE, BLK), BF),
         vmem((n2, HALF), BF),
         vmem((2, 4, TH, HALF), BF),
@@ -505,11 +600,17 @@
         vmem((2, 5, TH, HALF), F32),
         vmem((2, 5, TH, HALF), BF),
         vmem((2, 5, TH, HALF), BF),
+        vmem((HALF + TH, HALF), BF),
+        vmem((5, 4, TH, HALF), BF),
+        vmem((5, 2, 4, TH, HALF), BF),
+        vmem((2, 4, TH, HALF), F32),
+        vmem((4, TH, HALF), BF), vmem((4, TH, HALF), BF),
+        vmem((4, TH, HALF), BF), vmem((4, TH, HALF), BF),
         dma((5,)), dma((4, 3)),
         dma((5,)), dma((SPAN + 1,)), dma((5,)), dma((3,)), dma((4,)), dma, dma, dma, dma,
         dma((2, 2)), dma((4,)), dma((5, 2)), dma((5,)), dma((2, 2)), dma((4,)),
         dma, dma, dma, dma,
-        dma((4,)), dma((2, 2)), dma((4,)), dma((2, 2)),
+        dma((4,)), dma((2, 2)), dma((5,)), dma((5, 2)), dma, dma, dma((3,)), dma((4,)),
         dma((2, 4)), dma((2, 4)), dma((2, 5)), dma((2, 5)),
     ]
     any_spec = pl.BlockSpec(memory_space=pl.ANY)
@@ -520,7 +621,7 @@
         out_specs=pl.BlockSpec(memory_space=pltpu.VMEM),
         scratch_shapes=scratch,
         compiler_params=pltpu.CompilerParams(
-            collective_id=0, has_side_effects=True, vmem_limit_bytes=67_000_000
+            collective_id=0, has_side_effects=True, vmem_limit_bytes=56_300_000
         ),
         name="object_gradient",
     )(row_offsets, position_counts, object_slab, probe_wave, amplitudes, near, far)

time: 60.7 us -> 50.7 us (0.84)
  the two profiles are of different devices: /device:TPU:6 before, /device:TPU:392 now
where the time goes in v3:
time: 50.7 us; the launch traced here: 50.5 us
  Pallas kernels  49.2 us (97%)
  between operations  0.68 us (1%)
  local copies, waits for them, and re-layouts  0.66 us (1%)
    pallas_call x1, Pallas kernels, shards(): pl.pallas_call(functools.partial(body, tiles), out_shape=jax.ShapeDtypeSt...  49.2 us

profile of v3, /device:TPU:392, one launch (start us, length us, event | category | flops | bytes accessed | tf_op | source)
XLA Modules:
  0.0 50.5 jit_solution(16410651768415583373)
XLA Ops:
  0.0 0.0 copy-start
  0.7 0.0 copy-done
  0.7 49.2 %object_gradient.1 = f32[2,2,64,128]{3,2,1,0:T(8,128)S(1)} custom-call(s32[2]{0:T(128)S(1)} %copy-done, s32[1]{0:T(128)S(6)} %copy.9.cnt_hbm, f32[2,2,64,128]{3,2,1,0:T(8,128)} %slab_hbm.1, bf16[2,512,128]{2,1,0:T(8,128)(2,1)} %probe_hbm.1, f32[2,128,512]{2,1,0:T(8,128)} %amp_hbm.1, bf16[2,512,512]{2,1,0:T(8,128)(2,1)} %constant.4.clone.tq_hbm, ...), custom_call_target="tpu_custom_call" | custom-call | tf_op jit(solution)/shard_map/object_gradient/pallas_call | solution.py:617
  49.9 0.7 %copy.10 = f32[2,2,64,128]{3,2,1,0:T(8,128)} copy(f32[2,2,64,128]{3,2,1,0:T(8,128)S(1)} %object_gradient.1) | data formatting | bytes 262144
Async XLA Ops:
  0.0 0.7 %copy-start = (s32[2]{0:T(128)S(1)}, s32[2]{0:T(128)}, u32[]{:S(2)}) copy-start(s32[2]{0:T(128)} %off_hbm.1) | copy-start | bytes 28

commit v4 on v3

--- a/solution.py
+++ b/solution.py
@@ -45,7 +45,7 @@
     off_ref, cnt_ref, slab, probe, ampf, aq, bq, af, bf,
     win, o2g, o2w, offb, sel, psel, put, h1, ampb, hr, o2r, amp,
     ps, ew, gs, x1, ch, ks, y, t2s, gw, b2s, b2r, tp, odd, got, even, outs, oin,
-    pput, t2o, rin, acc, uo, ui, xo, xi,
+    pput, t2o, rin, acc, uo, ux, us, ui, xo, xi, mine,
     loc_sem, tab_sem,
     in_ss, in_rs, fw_ss, og_ss, og_rs, up_ss, up_rs, of_ss, of_rs,
     h1_ss, h1_rs, o2_ss, o2_rs, am_ss, am_rs,
@@ -147,11 +147,11 @@
 
     @pl.when(jnp.logical_not(above(8)))
     def _():
-        o2g[1] = jnp.zeros((4, TH, HALF), BF)
+        o2g[1, x] = jnp.zeros((TH, HALF), BF)
 
     @pl.when(jnp.logical_not(below(8)))
     def _():
-        ui[...] = jnp.zeros((4, TH, HALF), BF)
+        ui[...] = jnp.zeros((TH, HALF), BF)
 
     pl.semaphore_wait(
         barrier, 13 + jnp.minimum(4, (tiles - 1 - t) // 2) + jnp.minimum(4, t // 2))
@@ -176,6 +176,8 @@
         start(remote(
             win.at[0], win.at[k], in_ss.at[k // 2], in_rs.at[k], t - k, x), below(k))
 
+    start(remote(o2g.at[0, x], o2g.at[1, x], up_ss, up_rs, t - 8, x), below(8))
+
     def pass_on(m):
         k = 2 * m - 1 + 2 * c
         return remote(win.at[2 * m], win.at[k], fw_ss.at[m], in_rs.at[k], pair + d, x)
@@ -184,10 +186,18 @@
     def _():
         pass_on(0).start()
 
-    for step in range(1, 4):
-        start(remote(
-            o2g.at[0, x], o2g.at[0, x], og_ss.at[step - 1], og_rs.at[x],
-            t, lax.rem(x + step, 4)))
+    def gather(source):
+        for step in range(1, 4):
+            start(remote(
+                o2g.at[source, x], o2g.at[source, x], og_ss.at[source, step - 1],
+                og_rs.at[source, x], t, lax.rem(x + step, 4)))
+
+    def gathered(source):
+        for step in range(1, 4):
+            other = lax.rem(x + step, 4)
+            receive(o2g.at[source, other], og_rs.at[source, other])
+
+    gather(0)
     start(remote(offb.at[c], offb.at[c], of_ss, of_rs, pair + d, x))
 
     for s in range(2):
@@ -268,30 +278,31 @@
                     def _():
                         copy().start() if local else copy().wait_send()
 
-    for step in range(1, 4):
-        other = lax.rem(x + step, 4)
-        receive(o2g.at[0, other], og_rs.at[other])
-    start(remote(o2g.at[0], o2g.at[1], up_ss, up_rs, t - 8, x), below(8))
+    def take_tile(m, here, exists=None):
+        receive(win.at[2 * m], in_rs.at[2 * m], here if exists is None else jnp.logical_and(here, exists))
+
+        @pl.when(jnp.logical_and(here, jnp.logical_or(c == 0, m < 4)))
+        def _():
+            pass_on(m).start()
+
+    for m in range(1, 4):
+        take_tile(m, row + m <= 3)
+    for m in range(1, 5):
+        take_tile(m, row + m > 3, above(2 * m))
+    receive(o2g.at[1, x], up_rs, above(8))
+    gather(1)
+    gathered(0)
     for m in range(4):
         for r in range(2):
             plane_send(m, r, (0,), True)
-
-    def window():
-        for m in range(1, 5):
-            receive(win.at[2 * m], in_rs.at[2 * m], above(2 * m))
-
-            @pl.when(jnp.logical_or(c == 0, m < 4))
-            def _():
-                pass_on(m).start()
-        for k in range(1, SPAN + 1, 2):
-            receive(win.at[k], in_rs.at[k])
-        return jnp.concatenate([win[k] for k in range(SPAN + 1)], axis=0)
 
     def dot(left, right):
         return jnp.dot(left, right, preferred_element_type=F32)
 
     loads[2].wait()
-    wide = window()
+    for k in range(1, SPAN + 1, 2):
+        receive(win.at[k], in_rs.at[k])
+    wide = jnp.concatenate([win[k] for k in range(SPAN + 1)], axis=0)
     psi = []
     for s in range(2):
         patch = dot(sel[s], wide)
@@ -309,7 +320,7 @@
         for s in range(2):
             spread(*h1_of(s, r))
 
-    receive(o2g.at[1], up_rs, above(8))
+    gathered(1)
     for m in range(1, 5):
         for r in range(2):
             plane_send(m, r, (1,), True)
@@ -364,14 +375,20 @@
     for part in range(2):
         at = pl.multiple_of(part * P_SIZE + c * HALF, HALF)
         x1[c, part] = dot(ew[...], bf[:, pl.ds(at, HALF)]).astype(BF)
+    def near_rows(which, at):
+        left = jnp.concatenate([
+            af[at:at + HALF, pl.ds(pl.multiple_of(part * P_SIZE + which * HALF, HALF), HALF)]
+            for part in range(2)], axis=1)
+        return dot(left, jnp.concatenate([x1[which, part] for part in range(2)], axis=0))
+
+    for n in range(4):
+        mine[n] = near_rows(c, n * HALF)
     for n in range(4):
         receive(amp.at[n], am_rs.at[n])
     receive(x1.at[d], e1_rs)
-
-    right = jnp.concatenate([x1[r, part] for part in range(2) for r in range(2)], axis=0)
     for r in range(2):
-        fr = dot(af[r * HALF:(r + 1) * HALF, :], right)
-        fi = dot(af[P_SIZE + r * HALF:P_SIZE + (r + 1) * HALF, :], right)
+        fr = mine[r] + near_rows(d, r * HALF)
+        fi = mine[2 + r] + near_rows(d, P_SIZE + r * HALF)
         measured = jnp.concatenate([amp[2 * r], amp[2 * r + 1]], axis=0).astype(F32)
         keeping = 1.0 - measured / jnp.sqrt(fr * fr + fi * fi + smooth)
         ch[r * HALF:(r + 1) * HALF, :] = (fr * keeping).astype(BF)
@@ -385,12 +402,18 @@
     for part in range(2):
         at = pl.multiple_of(part * P_SIZE + c * HALF, HALF)
         y[c, part] = dot(bf[pl.ds(at, HALF), :], ch[...]).astype(BF)
+    def near_columns(which, at):
+        right = jnp.concatenate([
+            af[pl.ds(pl.multiple_of(part * P_SIZE + which * HALF, HALF), HALF), at:at + HALF]
+            for part in range(2)], axis=0)
+        return dot(jnp.concatenate([y[which, part] for part in range(2)], axis=1), right)
+
+    for n in range(4):
+        mine[n] = near_columns(c, n * HALF)
     receive(y.at[d], e2_rs)
-
-    left = jnp.concatenate([y[h, part] for part in range(2) for h in range(2)], axis=1)
     for h in range(2):
-        er = dot(left, af[:, h * HALF:(h + 1) * HALF])
-        ei = dot(left, af[:, P_SIZE + h * HALF:P_SIZE + (h + 1) * HALF])
+        er = mine[h] + near_columns(d, h * HALF)
+        ei = mine[2 + h] + near_columns(d, P_SIZE + h * HALF)
         wr, wi = ps[0, h].astype(F32), ps[1, h].astype(F32)
         sr, si = second(0, h), second(1, h)
         tr, ti = (wr * er + wi * ei).astype(BF), (wr * ei - wi * er).astype(BF)
@@ -465,12 +488,6 @@
                 b2s[2 * h + n, part] = back2[:, n * BLK:(n + 1) * BLK]
         for n in range(2):
             give(b2s, b2r, b2_ss, b2_rs, 2 * h + n)
-
-    for m in reversed(range(1, 5)):
-        for r in range(2):
-            term_take(m, r, 1)
-    uo[...] = acc[1].astype(BF)
-    start(remote(uo, ui, uu_ss, uu_rs, t + 8, x), above(8))
 
     for s in range(2):
         for r in range(2):
@@ -511,16 +528,29 @@
                 out_rs.at[which, m], t + 2 * m, x), above(2 * m))
 
     collect(0, tp[...])
+    for m in reversed(range(1, 5)):
+        for r in range(2):
+            term_take(m, r, 1)
+    uo[...] = acc[1].astype(BF)
+    for step in range(1, 4):
+        other = lax.rem(x + step, 4)
+        start(remote(uo.at[other], ux.at[x], xs_ss.at[1, step - 1], xs_rs.at[1, x], t, other))
     hand_on(0)
     for m in range(4):
         for r in range(2):
             term_take(m, r, 0)
-    receive(ui, uu_rs, below(8))
-    acc[0] += ui[...].astype(F32)
     xo[...] = acc[0].astype(BF)
     for step in range(1, 4):
         other = lax.rem(x + step, 4)
-        start(remote(xo.at[other], xi.at[x], xs_ss.at[step - 1], xs_rs.at[x], t, other))
+        start(remote(xo.at[other], xi.at[x], xs_ss.at[0, step - 1], xs_rs.at[0, x], t, other))
+
+    total = acc[1, x]
+    for step in range(1, 4):
+        other = lax.rem(x + step, 4)
+        receive(ux.at[other], xs_rs.at[1, other])
+        total = total + ux[other].astype(F32)
+    us[...] = total.astype(BF)
+    start(remote(us, ui, uu_ss, uu_rs, t + 8, x), above(8))
 
     total = even[0, 0]
     for m in range(1, 5):
@@ -532,8 +562,10 @@
     total = acc[0, x]
     for step in range(1, 4):
         other = lax.rem(x + step, 4)
-        receive(xi.at[other], xs_rs.at[other])
+        receive(xi.at[other], xs_rs.at[0, other])
         total = total + xi[other].astype(F32)
+    receive(ui, uu_rs, below(8))
+    total = total + ui[...].astype(F32)
     for part in range(2):
         out_ref[1, part] = total[:, part * BLK:(part + 1) * BLK]
 
@@ -605,12 +637,14 @@
         vmem((5, 2, 4, TH, HALF), BF),
         vmem((2, 4, TH, HALF), F32),
         vmem((4, TH, HALF), BF), vmem((4, TH, HALF), BF),
+        vmem((TH, HALF), BF), vmem((TH, HALF), BF),
         vmem((4, TH, HALF), BF), vmem((4, TH, HALF), BF),
+        vmem((4, HALF, HALF), F32),
         dma((5,)), dma((4, 3)),
-        dma((5,)), dma((SPAN + 1,)), dma((5,)), dma((3,)), dma((4,)), dma, dma, dma, dma,
+        dma((5,)), dma((SPAN + 1,)), dma((5,)), dma((2, 3)), dma((2, 4)), dma, dma, dma, dma,
         dma((2, 2)), dma((4,)), dma((5, 2)), dma((5,)), dma((2, 2)), dma((4,)),
         dma, dma, dma, dma,
-        dma((4,)), dma((2, 2)), dma((5,)), dma((5, 2)), dma, dma, dma((3,)), dma((4,)),
+        dma((4,)), dma((2, 2)), dma((5,)), dma((5, 2)), dma, dma, dma((2, 3)), dma((2, 4)),
         dma((2, 4)), dma((2, 4)), dma((2, 5)), dma((2, 5)),
     ]
     any_spec = pl.BlockSpec(memory_space=pl.ANY)

time: 50.7 us -> 50.7 us (level)
  the two profiles are of different devices: /device:TPU:392 before, /device:TPU:384 now
where the time goes in v4:
time: 50.7 us; the launch traced here: 50.5 us
  Pallas kernels  49.2 us (97%)
  between operations  0.68 us (1%)
  local copies, waits for them, and re-layouts  0.66 us (1%)
    pallas_call x1, Pallas kernels, shards(): pl.pallas_call(functools.partial(body, tiles), out_shape=jax.ShapeDtypeSt...  49.2 us

profile of v4, /device:TPU:384, one launch (start us, length us, event | category | flops | bytes accessed | tf_op | source)
XLA Modules:
  0.0 50.5 jit_solution(2783356584959355454)
XLA Ops:
  0.0 0.0 copy-start
  0.7 0.0 copy-done
  0.7 49.2 %object_gradient.1 = f32[2,2,64,128]{3,2,1,0:T(8,128)S(1)} custom-call(s32[2]{0:T(128)S(1)} %copy-done, s32[1]{0:T(128)S(6)} %copy.9.cnt_hbm, f32[2,2,64,128]{3,2,1,0:T(8,128)} %slab_hbm.1, bf16[2,512,128]{2,1,0:T(8,128)(2,1)} %probe_hbm.1, f32[2,128,512]{2,1,0:T(8,128)} %amp_hbm.1, bf16[2,512,512]{2,1,0:T(8,128)(2,1)} %constant.4.clone.tq_hbm, ...), custom_call_target="tpu_custom_call" | custom-call | tf_op jit(solution)/shard_map/object_gradient/pallas_call | solution.py:651
  49.9 0.7 %copy.10 = f32[2,2,64,128]{3,2,1,0:T(8,128)} copy(f32[2,2,64,128]{3,2,1,0:T(8,128)S(1)} %object_gradient.1) | data formatting | bytes 262144
Async XLA Ops:
  0.0 0.7 %copy-start = (s32[2]{0:T(128)S(1)}, s32[2]{0:T(128)}, u32[]{:S(2)}) copy-start(s32[2]{0:T(128)} %off_hbm.1) | copy-start | bytes 28

commit v5 on v4

--- a/solution.py
+++ b/solution.py
@@ -287,10 +287,10 @@
 
     for m in range(1, 4):
         take_tile(m, row + m <= 3)
+    receive(o2g.at[1, x], up_rs, above(8))
+    gather(1)
     for m in range(1, 5):
         take_tile(m, row + m > 3, above(2 * m))
-    receive(o2g.at[1, x], up_rs, above(8))
-    gather(1)
     gathered(0)
     for m in range(4):
         for r in range(2):

time: 50.7 us -> 50.6 us (level)
  no operation moved by 1% of the time
where the time goes in v5:
time: 50.6 us; the launch traced here: 50.5 us
  Pallas kernels  49.2 us (97%)
  between operations  0.68 us (1%)
  local copies, waits for them, and re-layouts  0.66 us (1%)
    pallas_call x1, Pallas kernels, shards(): pl.pallas_call(functools.partial(body, tiles), out_shape=jax.ShapeDtypeSt...  49.2 us

profile of v5, /device:TPU:384, one launch (start us, length us, event | category | flops | bytes accessed | tf_op | source)
XLA Modules:
  0.0 50.5 jit_solution(10661092449633576725)
XLA Ops:
  0.0 0.0 copy-start
  0.7 0.0 copy-done
  0.7 49.2 %object_gradient.1 = f32[2,2,64,128]{3,2,1,0:T(8,128)S(1)} custom-call(s32[2]{0:T(128)S(1)} %copy-done, s32[1]{0:T(128)S(6)} %copy.9.cnt_hbm, f32[2,2,64,128]{3,2,1,0:T(8,128)} %slab_hbm.1, bf16[2,512,128]{2,1,0:T(8,128)(2,1)} %probe_hbm.1, f32[2,128,512]{2,1,0:T(8,128)} %amp_hbm.1, bf16[2,512,512]{2,1,0:T(8,128)(2,1)} %constant.4.clone.tq_hbm, ...), custom_call_target="tpu_custom_call" | custom-call | tf_op jit(solution)/shard_map/object_gradient/pallas_call | solution.py:651
  49.9 0.7 %copy.10 = f32[2,2,64,128]{3,2,1,0:T(8,128)} copy(f32[2,2,64,128]{3,2,1,0:T(8,128)S(1)} %object_gradient.1) | data formatting | bytes 262144
Async XLA Ops:
  0.0 0.7 %copy-start = (s32[2]{0:T(128)S(1)}, s32[2]{0:T(128)}, u32[]{:S(2)}) copy-start(s32[2]{0:T(128)} %off_hbm.1) | copy-start | bytes 28
